TPU v7x, 512 devices: a whole 4x4x16 slice. The times are simulated.
512 devices in a mesh: dom: 128 (over x, z, core), blk: 4 (over y).
Axes of the slice: x: 4, y: 4, z: 16, core: 2. Of those that a mesh axis runs over, the one named last changes fastest.
Arguments:
- degree: int32 [1024], P('dom'), may hold values from 1 to 3
- face_elem: int32 [4096], P('dom'), may hold values from 0 to 7
- face_side: int32 [4096], P('dom'), may hold values from 0 to 8, as said below
- face_peer: int32 [4096], P('dom'), may hold values from 0 to 7
- coupling: bfloat16 [4096, 320, 320], P('dom', 'blk'), may hold values from -0.078125 to 0.078125
- inv_diag: float32 [1024, 320], P('dom', 'blk'), may hold values from 0.5 to 2
- inv_off: bfloat16 [1024, 320, 320], P('dom', 'blk'), may hold values from -0.109375 to 0.109375
- source: float32 [1024, 320], P('dom', 'blk'), may hold values from -6 to 6
- residual: float32 [1024, 320], P('dom', 'blk'), may hold values from -0.6 to 0.6
Outputs:
- adjoint: float32 [1024, 320], P('dom', 'blk')
- indicator: float32 [1024], P('dom')
Inputs may be any that keep to these rules, and one draw needn't show every extreme that they name: `face_side`: among the 32 faces of one partition (aligned blocks of 32 rows) each side from 1 to 8 is named by at least 2 and at most 4 faces, and one side by exactly 4; the remaining faces have side 0.
All inputs are finite; a program needn't handle non-finite values.
Results may differ from a plain program's by a relative error of at most 0.004.
Values may be sent and summed in bfloat16 or wider, within the bound.
No kernel may reach another device: no remote copies, remote signals or barrier semaphores. Data moves between devices by JAX's collectives and lax.ppermute only.
A program may use at most 64 MiB of HBM per device.

v0:
```python
import jax
import jax.numpy as jnp
from jax import lax
from jax.sharding import PartitionSpec as P

MODES = 64
SWEEPS = 2
NEIGH = 8


def from_behind(block, axis, distance):
    devices = range(lax.axis_size(axis))
    route = [((i - distance) % len(devices), i) for i in devices]
    return lax.ppermute(block, axis, route)


def full_rows(values):
    return lax.all_gather(values, "blk", axis=1, tiled=True)


def local(degree, face_elem, face_side, face_peer, coupling, inv_diag, inv_off, source, residual):
    width = coupling.shape[2]
    quarter = source.shape[1]
    elements = source.shape[0]
    faces = coupling.shape[0]
    neigh = NEIGH
    half_count = neigh // 2
    capacity = faces // neigh
    offsets = [step_size for step_size in range(1, half_count + 1)] + [
        -step_size for step_size in range(1, half_count + 1)
    ]
    first_row = lax.axis_index("blk") * quarter
    limit = (degree + 1) ** 3 * MODES // 64
    modes = jnp.arange(width, dtype=jnp.int32) % MODES
    mask_full = (modes[None, :] < limit[:, None]).astype(jnp.float32)
    mask_rows = lax.dynamic_slice_in_dim(mask_full, first_row, quarter, 1)
    codes = jnp.arange(neigh + 1, dtype=jnp.int32)
    onehot = (face_side[:, None] == codes[None, :]).astype(jnp.int32)
    before = jnp.cumsum(onehot, axis=0) - onehot
    slot_index = jnp.sum(before * onehot, axis=1)
    crossing = face_side > 0
    inner = jnp.where(crossing, 0.0, 1.0).astype(jnp.float32)
    position = jnp.where(crossing, (face_side - 1) * capacity + slot_index, neigh * capacity)
    safe_position = jnp.minimum(position, neigh * capacity - 1)
    wanted = (
        jnp.zeros((neigh * capacity,), jnp.int32)
        .at[position]
        .set(face_peer, mode="drop")
        .reshape(neigh, capacity)
    )
    requested = jnp.stack(
        [from_behind(wanted[side_num], "dom", offsets[side_num]) for side_num in range(neigh)]
    )
    requested_flat = requested.reshape(-1)

    def invert(values_full):
        own_part = lax.dynamic_slice_in_dim(values_full, first_row, quarter, 1)
        product = jnp.einsum("eij,ej->ei", inv_off, values_full, preferred_element_type=jnp.float32)
        return inv_diag * own_part.astype(jnp.float32) + product

    source_half = (source * mask_rows).astype(jnp.bfloat16)
    base_state = invert(full_rows(source_half)) * mask_rows
    adjoint = base_state
    for sweep_index in range(SWEEPS):
        state_rows = adjoint.astype(jnp.bfloat16)
        state_full = full_rows(state_rows)
        outgoing = state_full[requested]
        incoming = jnp.stack(
            [
                from_behind(outgoing[side_num], "dom", -offsets[side_num])
                for side_num in range(neigh)
            ]
        ).reshape(-1, width)
        peer_state = jnp.where(crossing[:, None], incoming[safe_position], state_full[face_peer])
        elem_state = state_rows[face_elem]
        local_terms = jnp.einsum(
            "fij,fj->fi", coupling, peer_state, preferred_element_type=jnp.float32
        )
        transposed = jnp.einsum(
            "fij,fi->fj", coupling, elem_state, preferred_element_type=jnp.float32
        )
        own_terms = jnp.zeros((elements, quarter), jnp.float32).at[face_elem].add(local_terms)
        partial_value = (
            jnp.zeros((elements, width), jnp.float32).at[face_peer].add(transposed * inner[:, None])
        )
        outbound = (
            jnp.zeros((neigh * capacity, width), jnp.float32)
            .at[position]
            .set(transposed, mode="drop")
            .reshape(neigh, capacity, width)
        )
        returned = jnp.stack(
            [from_behind(outbound[side_num], "dom", offsets[side_num]) for side_num in range(neigh)]
        ).reshape(-1, width)
        partial_value = partial_value.at[requested_flat].add(returned)
        middle = lax.dynamic_slice_in_dim(partial_value, first_row, quarter, 1) + own_terms
        partial_value = lax.dynamic_update_slice_in_dim(partial_value, middle, first_row, 1)
        summed = lax.psum(partial_value, "blk")
        coupled_half = (summed * mask_full).astype(jnp.bfloat16)
        adjoint = (base_state - invert(coupled_half)) * mask_rows
    weights = jnp.sum(adjoint * residual * mask_rows, axis=1)
    indicator = lax.psum(weights, "blk")
    return (adjoint, indicator)


def solution(mesh):
    in_specs = (
        P("dom"),
        P("dom"),
        P("dom"),
        P("dom"),
        P("dom", "blk", None),
        P("dom", "blk"),
        P("dom", "blk", None),
        P("dom", "blk"),
        P("dom", "blk"),
    )
    out_specs = (P("dom", "blk"), P("dom"))
    return jax.shard_map(local, mesh=mesh, in_specs=in_specs, out_specs=out_specs, check_vma=False)
```

profile of v0, /device:TPU:64, one launch (start us, length us, event | category | flops | bytes accessed | tf_op | source)
XLA Modules:
  0.0 313.2 jit_solution(9358824529545259234)
XLA Ops:
  5.9 3.8 %collective-permute-start.1 = (s32[4]{0:T(128)S(1)}, s32[4]{0:T(128)S(1)}, u32[]{:S(2)}, u32[]{:S(2)}) collective-permute-start(s32[4]{0:T(128)S(1)} %get-tuple-element.44), channel_id=1, source_target_pairs={{504,0},{508,4},{0,8},{4,12},{8,16},{12,20},{16,24},{20,28},{24,32... | collective-permute-start | bytes 56 | tf_op jit(solution)/shard_map/ppermute | solution.py:14
  9.7 6.4 %collective-permute-start.2 = (s32[4]{0:T(128)S(1)}, s32[4]{0:T(128)S(1)}, u32[]{:S(2)}, u32[]{:S(2)}) collective-permute-start(s32[4]{0:T(128)S(1)} %get-tuple-element.43), channel_id=1, source_target_pairs={{500,0},{504,4},{508,8},{0,12},{4,16},{8,20},{12,24},{16,28},{20,3... | collective-permute-start | bytes 56 | tf_op jit(solution)/shard_map/ppermute | solution.py:14
  16.1 5.2 %collective-permute-start.3 = (s32[4]{0:T(128)S(1)}, s32[4]{0:T(128)S(1)}, u32[]{:S(2)}, u32[]{:S(2)}) collective-permute-start(s32[4]{0:T(128)S(1)} %get-tuple-element.42), channel_id=1, source_target_pairs={{496,0},{500,4},{504,8},{508,12},{0,16},{4,20},{8,24},{12,28},{16,... | collective-permute-start | bytes 56 | tf_op jit(solution)/shard_map/ppermute | solution.py:14
  21.3 1.9 collective-permute-start.4
  26.7 11.3 %all-gather = bf16[4,80,8]{1,2,0:T(8,128)(2,1)S(1)} all-gather(bf16[1,80,8]{1,2,0:T(8,128)(2,1)S(1)} %fusion.36), channel_id=1, replica_groups=mesh['dom'=128,'blk'=4] {'blk'}, dimensions={0}, use_global_device_ids=true | all-gather | bytes 6400 | tf_op jit(solution)/shard_map/all_gather | solution.py:18
  43.5 10.4 %all-gather.1 = bf16[4,80,8]{1,2,0:T(8,128)(2,1)S(1)} all-gather(bf16[1,80,8]{1,2,0:T(8,128)(2,1)S(1)} %bitcast.165), channel_id=1, replica_groups=mesh['dom'=128,'blk'=4] {'blk'}, dimensions={0}, use_global_device_ids=true | all-gather | bytes 6400 | tf_op jit(solution)/shard_map/all_gather | solution.py:18
  54.7 2.0 collective-permute-start.5
  56.7 1.9 collective-permute-start.6
  58.7 5.2 %collective-permute-start.7 = (s32[4]{0:T(128)S(1)}, s32[4]{0:T(128)S(1)}, u32[]{:S(2)}, u32[]{:S(2)}) collective-permute-start(s32[4]{0:T(128)S(1)} %get-tuple-element.38), channel_id=1, source_target_pairs={{16,0},{20,4},{24,8},{28,12},{32,16},{36,20},{40,24},{44,28},{48,3... | collective-permute-start | bytes 56 | tf_op jit(solution)/shard_map/ppermute | solution.py:14
  63.9 3.5 %collective-permute-start.8 = (f32[4,320]{1,0:T(4,128)S(1)}, f32[4,320]{1,0:T(4,128)S(1)}, u32[]{:S(2)}, u32[]{:S(2)}) collective-permute-start(f32[4,320]{1,0:T(4,128)S(1)} %get-tuple-element.21), channel_id=1, source_target_pairs={{508,0},{0,4},{4,8},{8,12},{12,16},{16,20},{20,24},{24,28},{28,32}... | collective-permute-start | bytes 15368 | tf_op jit(solution)/shard_map/ppermute | solution.py:14
  67.4 2.2 collective-permute-start.9
  69.6 3.9 %collective-permute-start.10 = (f32[4,320]{1,0:T(4,128)S(1)}, f32[4,320]{1,0:T(4,128)S(1)}, u32[]{:S(2)}, u32[]{:S(2)}) collective-permute-start(f32[4,320]{1,0:T(4,128)S(1)} %get-tuple-element.19), channel_id=1, source_target_pairs={{500,0},{504,4},{508,8},{0,12},{4,16},{8,20},{12,24},{16,28},{20,3... | collective-permute-start | bytes 15368 | tf_op jit(solution)/shard_map/ppermute | solution.py:14
  73.6 4.8 %collective-permute-start.11 = (f32[4,320]{1,0:T(4,128)S(1)}, f32[4,320]{1,0:T(4,128)S(1)}, u32[]{:S(2)}, u32[]{:S(2)}) collective-permute-start(f32[4,320]{1,0:T(4,128)S(1)} %get-tuple-element.18), channel_id=1, source_target_pairs={{496,0},{500,4},{504,8},{508,12},{0,16},{4,20},{8,24},{12,28},{16,... | collective-permute-start | bytes 15368 | tf_op jit(solution)/shard_map/ppermute | solution.py:14
  79.4 2.2 collective-permute-start.16
  82.8 2.5 collective-permute-start.17
  85.3 3.1 collective-permute-done.17
  88.4 8.1 %collective-permute-start.18 = (bf16[4,320]{1,0:T(4,128)(2,1)S(1)}, bf16[4,320]{1,0:T(4,128)(2,1)S(1)}, u32[]{:S(2)}, u32[]{:S(2)}) collective-permute-start(bf16[4,320]{1,0:T(4,128)(2,1)S(1)} %get-tuple-element.35), channel_id=1, source_target_pairs={{12,0},{16,4},{20,8},{24,12},{28,16},{32,20},{36,24},{40,28},{44,3... | collective-permute-start | bytes 7688 | tf_op jit(solution)/shard_map/ppermute | solution.py:14
  97.8 3.6 %collective-permute-start.19 = (bf16[4,320]{1,0:T(4,128)(2,1)S(1)}, bf16[4,320]{1,0:T(4,128)(2,1)S(1)}, u32[]{:S(2)}, u32[]{:S(2)}) collective-permute-start(bf16[4,320]{1,0:T(4,128)(2,1)S(1)} %get-tuple-element.34), channel_id=1, source_target_pairs={{16,0},{20,4},{24,8},{28,12},{32,16},{36,20},{40,24},{44,28},{48,3... | collective-permute-start | bytes 7688 | tf_op jit(solution)/shard_map/ppermute | solution.py:14
  101.5 4.0 %collective-permute-done.19 = bf16[4,320]{1,0:T(4,128)(2,1)S(1)} collective-permute-done((bf16[4,320]{1,0:T(4,128)(2,1)S(1)}, bf16[4,320]{1,0:T(4,128)(2,1)S(1)}, u32[]{:S(2)}, u32[]{:S(2)}) %collective-permute-start.19) | collective-permute-done | bytes 2592 | tf_op jit(solution)/shard_map/ppermute | solution.py:14
  107.4 7.2 %collective-permute-done.20 = bf16[4,320]{1,0:T(4,128)(2,1)S(1)} collective-permute-done((bf16[4,320]{1,0:T(4,128)(2,1)S(1)}, bf16[4,320]{1,0:T(4,128)(2,1)S(1)}, u32[]{:S(2)}, u32[]{:S(2)}) %collective-permute-start.20) | collective-permute-done | bytes 2592 | tf_op jit(solution)/shard_map/ppermute | solution.py:14
  116.5 3.5 %collective-permute-done.21 = bf16[4,320]{1,0:T(4,128)(2,1)S(1)} collective-permute-done((bf16[4,320]{1,0:T(4,128)(2,1)S(1)}, bf16[4,320]{1,0:T(4,128)(2,1)S(1)}, u32[]{:S(2)}, u32[]{:S(2)}) %collective-permute-start.21) | collective-permute-done | bytes 2592 | tf_op jit(solution)/shard_map/ppermute | solution.py:14
  122.0 4.4 %collective-permute-done.22 = bf16[4,320]{1,0:T(4,128)(2,1)S(1)} collective-permute-done((bf16[4,320]{1,0:T(4,128)(2,1)S(1)}, bf16[4,320]{1,0:T(4,128)(2,1)S(1)}, u32[]{:S(2)}, u32[]{:S(2)}) %collective-permute-start.22) | collective-permute-done | bytes 2592 | tf_op jit(solution)/shard_map/ppermute | solution.py:14
  126.4 2.1 collective-permute-start.23
  128.6 13.6 %collective-permute-done.23 = bf16[4,320]{1,0:T(4,128)(2,1)S(1)} collective-permute-done((bf16[4,320]{1,0:T(4,128)(2,1)S(1)}, bf16[4,320]{1,0:T(4,128)(2,1)S(1)}, u32[]{:S(2)}, u32[]{:S(2)}) %collective-permute-start.23) | collective-permute-done | bytes 2592 | tf_op jit(solution)/shard_map/ppermute | solution.py:14
  145.6 3.4 %collective-permute-start.13 = (f32[4,320]{1,0:T(4,128)S(1)}, f32[4,320]{1,0:T(4,128)S(1)}, u32[]{:S(2)}, u32[]{:S(2)}) collective-permute-start(f32[4,320]{1,0:T(4,128)S(1)} %get-tuple-element.16), channel_id=1, source_target_pairs={{8,0},{12,4},{16,8},{20,12},{24,16},{28,20},{32,24},{36,28},{40,32... | collective-permute-start | bytes 15368 | tf_op jit(solution)/shard_map/ppermute | solution.py:14
  149.0 6.8 %collective-permute-start.14 = (f32[4,320]{1,0:T(4,128)S(1)}, f32[4,320]{1,0:T(4,128)S(1)}, u32[]{:S(2)}, u32[]{:S(2)}) collective-permute-start(f32[4,320]{1,0:T(4,128)S(1)} %get-tuple-element.15), channel_id=1, source_target_pairs={{12,0},{16,4},{20,8},{24,12},{28,16},{32,20},{36,24},{40,28},{44,3... | collective-permute-start | bytes 15368 | tf_op jit(solution)/shard_map/ppermute | solution.py:14
  155.9 1.9 collective-permute-start.15
  157.9 5.6 %collective-permute-done.15 = f32[4,320]{1,0:T(4,128)S(1)} collective-permute-done((f32[4,320]{1,0:T(4,128)S(1)}, f32[4,320]{1,0:T(4,128)S(1)}, u32[]{:S(2)}, u32[]{:S(2)}) %collective-permute-start.15) | collective-permute-done | bytes 5152 | tf_op jit(solution)/shard_map/ppermute | solution.py:14
  165.4 15.8 %psum.21 = bf16[8,320]{1,0:T(8,128)(2,1)S(1)} all-reduce(f32[8,320]{1,0:T(8,128)S(1)} %dynamic_update_slice.6), channel_id=1, replica_groups=mesh['dom'=128,'blk'=4] {'blk'}, use_global_device_ids=true, to_apply=%region_7.8 | all-reduce | flops 2560 | bytes 15360 | tf_op jit(solution)/shard_map/psum | solution.py:98
  183.4 10.4 %all-gather.2 = bf16[4,80,8]{1,2,0:T(8,128)(2,1)S(1)} all-gather(bf16[1,80,8]{1,2,0:T(8,128)(2,1)S(1)} %bitcast.166), channel_id=1, replica_groups=mesh['dom'=128,'blk'=4] {'blk'}, dimensions={0}, use_global_device_ids=true | all-gather | bytes 6400 | tf_op jit(solution)/shard_map/all_gather | solution.py:18
  198.0 2.4 collective-permute-start.24
  200.5 3.6 %collective-permute-start.25 = (f32[4,320]{1,0:T(4,128)S(1)}, f32[4,320]{1,0:T(4,128)S(1)}, u32[]{:S(2)}, u32[]{:S(2)}) collective-permute-start(f32[4,320]{1,0:T(4,128)S(1)} %get-tuple-element.12), channel_id=1, source_target_pairs={{504,0},{508,4},{0,8},{4,12},{8,16},{12,20},{16,24},{20,28},{24,32... | collective-permute-start | bytes 15368 | tf_op jit(solution)/shard_map/ppermute | solution.py:14
  204.1 1.9 collective-permute-start.26
  208.0 3.4 %collective-permute-start.33 = (bf16[4,320]{1,0:T(4,128)(2,1)S(1)}, bf16[4,320]{1,0:T(4,128)(2,1)S(1)}, u32[]{:S(2)}, u32[]{:S(2)}) collective-permute-start(bf16[4,320]{1,0:T(4,128)(2,1)S(1)} %get-tuple-element.28), channel_id=1, source_target_pairs={{8,0},{12,4},{16,8},{20,12},{24,16},{28,20},{32,24},{36,28},{40,32... | collective-permute-start | bytes 7688 | tf_op jit(solution)/shard_map/ppermute | solution.py:14
  211.4 2.1 collective-permute-done.33
  213.5 5.9 %collective-permute-start.34 = (bf16[4,320]{1,0:T(4,128)(2,1)S(1)}, bf16[4,320]{1,0:T(4,128)(2,1)S(1)}, u32[]{:S(2)}, u32[]{:S(2)}) collective-permute-start(bf16[4,320]{1,0:T(4,128)(2,1)S(1)} %get-tuple-element.27), channel_id=1, source_target_pairs={{12,0},{16,4},{20,8},{24,12},{28,16},{32,20},{36,24},{40,28},{44,3... | collective-permute-start | bytes 7688 | tf_op jit(solution)/shard_map/ppermute | solution.py:14
  220.7 5.3 %collective-permute-start.35 = (bf16[4,320]{1,0:T(4,128)(2,1)S(1)}, bf16[4,320]{1,0:T(4,128)(2,1)S(1)}, u32[]{:S(2)}, u32[]{:S(2)}) collective-permute-start(bf16[4,320]{1,0:T(4,128)(2,1)S(1)} %get-tuple-element.26), channel_id=1, source_target_pairs={{16,0},{20,4},{24,8},{28,12},{32,16},{36,20},{40,24},{44,28},{48,3... | collective-permute-start | bytes 7688 | tf_op jit(solution)/shard_map/ppermute | solution.py:14
  226.0 2.2 collective-permute-done.35
  228.3 3.1 collective-permute-start.36
  231.4 6.0 %collective-permute-done.36 = bf16[4,320]{1,0:T(4,128)(2,1)S(1)} collective-permute-done((bf16[4,320]{1,0:T(4,128)(2,1)S(1)}, bf16[4,320]{1,0:T(4,128)(2,1)S(1)}, u32[]{:S(2)}, u32[]{:S(2)}) %collective-permute-start.36) | collective-permute-done | bytes 2592 | tf_op jit(solution)/shard_map/ppermute | solution.py:14
  239.3 4.8 %collective-permute-done.37 = bf16[4,320]{1,0:T(4,128)(2,1)S(1)} collective-permute-done((bf16[4,320]{1,0:T(4,128)(2,1)S(1)}, bf16[4,320]{1,0:T(4,128)(2,1)S(1)}, u32[]{:S(2)}, u32[]{:S(2)}) %collective-permute-start.37) | collective-permute-done | bytes 2592 | tf_op jit(solution)/shard_map/ppermute | solution.py:14
  246.1 4.6 %collective-permute-done.38 = bf16[4,320]{1,0:T(4,128)(2,1)S(1)} collective-permute-done((bf16[4,320]{1,0:T(4,128)(2,1)S(1)}, bf16[4,320]{1,0:T(4,128)(2,1)S(1)}, u32[]{:S(2)}, u32[]{:S(2)}) %collective-permute-start.38) | collective-permute-done | bytes 2592 | tf_op jit(solution)/shard_map/ppermute | solution.py:14
  252.7 12.3 %collective-permute-done.39 = bf16[4,320]{1,0:T(4,128)(2,1)S(1)} collective-permute-done((bf16[4,320]{1,0:T(4,128)(2,1)S(1)}, bf16[4,320]{1,0:T(4,128)(2,1)S(1)}, u32[]{:S(2)}, u32[]{:S(2)}) %collective-permute-start.39) | collective-permute-done | bytes 2592 | tf_op jit(solution)/shard_map/ppermute | solution.py:14
  268.4 3.4 %collective-permute-start.29 = (f32[4,320]{1,0:T(4,128)S(1)}, f32[4,320]{1,0:T(4,128)S(1)}, u32[]{:S(2)}, u32[]{:S(2)}) collective-permute-start(f32[4,320]{1,0:T(4,128)S(1)} %get-tuple-element.8), channel_id=1, source_target_pairs={{8,0},{12,4},{16,8},{20,12},{24,16},{28,20},{32,24},{36,28},{40,32... | collective-permute-start | bytes 15368 | tf_op jit(solution)/shard_map/ppermute | solution.py:14
  271.9 6.8 %collective-permute-start.30 = (f32[4,320]{1,0:T(4,128)S(1)}, f32[4,320]{1,0:T(4,128)S(1)}, u32[]{:S(2)}, u32[]{:S(2)}) collective-permute-start(f32[4,320]{1,0:T(4,128)S(1)} %get-tuple-element.7), channel_id=1, source_target_pairs={{12,0},{16,4},{20,8},{24,12},{28,16},{32,20},{36,24},{40,28},{44,3... | collective-permute-start | bytes 15368 | tf_op jit(solution)/shard_map/ppermute | solution.py:14
  280.7 5.6 %collective-permute-done.31 = f32[4,320]{1,0:T(4,128)S(1)} collective-permute-done((f32[4,320]{1,0:T(4,128)S(1)}, f32[4,320]{1,0:T(4,128)S(1)}, u32[]{:S(2)}, u32[]{:S(2)}) %collective-permute-start.31) | collective-permute-done | bytes 5152 | tf_op jit(solution)/shard_map/ppermute | solution.py:14
  288.2 14.3 %psum.22 = bf16[8,320]{1,0:T(8,128)(2,1)S(1)} all-reduce(f32[8,320]{1,0:T(8,128)S(1)} %dynamic_update_slice.7), channel_id=1, replica_groups=mesh['dom'=128,'blk'=4] {'blk'}, use_global_device_ids=true, to_apply=%region_12.13 | all-reduce | flops 2560 | bytes 15360 | tf_op jit(solution)/shard_map/psum | solution.py:98
  303.7 9.5 %psum.23 = f32[8]{0:T(128)} all-reduce(f32[8]{0:T(128)S(1)} %get-tuple-element.2), channel_id=1, replica_groups=mesh['dom'=128,'blk'=4] {'blk'}, use_global_device_ids=true, to_apply=%region_14.15 | all-reduce | flops 8 | bytes 64 | tf_op jit(solution)/shard_map/psum | solution.py:102
  (160 shorter events, 53.5 us)
Async XLA Ops:
  0.6 40.9 %copy-start = (bf16[32,80,320]{2,1,0:T(8,128)(2,1)S(1)}, bf16[32,80,320]{2,1,0:T(8,128)(2,1)}, u32[]{:S(2)}) copy-start(bf16[32,80,320]{2,1,0:T(8,128)(2,1)} %param.13) | copy-start | bytes 4915204
  4.0 50.7 %collective-permute-start = (s32[4]{0:T(128)S(1)}, s32[4]{0:T(128)S(1)}, u32[]{:S(2)}, u32[]{:S(2)}) collective-permute-start(s32[4]{0:T(128)S(1)} %get-tuple-element.45), channel_id=1, source_target_pairs={{508,0},{0,4},{4,8},{8,12},{12,16},{16,20},{20,24},{24,28},{28,32}... | collective-permute-start | bytes 56 | tf_op jit(solution)/shard_map/ppermute | solution.py:14
  5.9 50.8 %collective-permute-start.1 = (s32[4]{0:T(128)S(1)}, s32[4]{0:T(128)S(1)}, u32[]{:S(2)}, u32[]{:S(2)}) collective-permute-start(s32[4]{0:T(128)S(1)} %get-tuple-element.44), channel_id=1, source_target_pairs={{504,0},{508,4},{0,8},{4,12},{8,16},{12,20},{16,24},{20,28},{24,32... | collective-permute-start | bytes 56 | tf_op jit(solution)/shard_map/ppermute | solution.py:14
  9.7 48.9 %collective-permute-start.2 = (s32[4]{0:T(128)S(1)}, s32[4]{0:T(128)S(1)}, u32[]{:S(2)}, u32[]{:S(2)}) collective-permute-start(s32[4]{0:T(128)S(1)} %get-tuple-element.43), channel_id=1, source_target_pairs={{500,0},{504,4},{508,8},{0,12},{4,16},{8,20},{12,24},{16,28},{20,3... | collective-permute-start | bytes 56 | tf_op jit(solution)/shard_map/ppermute | solution.py:14
  16.1 47.8 %collective-permute-start.3 = (s32[4]{0:T(128)S(1)}, s32[4]{0:T(128)S(1)}, u32[]{:S(2)}, u32[]{:S(2)}) collective-permute-start(s32[4]{0:T(128)S(1)} %get-tuple-element.42), channel_id=1, source_target_pairs={{496,0},{500,4},{504,8},{508,12},{0,16},{4,20},{8,24},{12,28},{16,... | collective-permute-start | bytes 56 | tf_op jit(solution)/shard_map/ppermute | solution.py:14
  21.3 46.1 %collective-permute-start.4 = (s32[4]{0:T(128)S(1)}, s32[4]{0:T(128)S(1)}, u32[]{:S(2)}, u32[]{:S(2)}) collective-permute-start(s32[4]{0:T(128)S(1)} %get-tuple-element.41), channel_id=1, source_target_pairs={{4,0},{8,4},{12,8},{16,12},{20,16},{24,20},{28,24},{32,28},{36,32}... | collective-permute-start | bytes 56 | tf_op jit(solution)/shard_map/ppermute | solution.py:14
  54.7 14.9 %collective-permute-start.5 = (s32[4]{0:T(128)S(1)}, s32[4]{0:T(128)S(1)}, u32[]{:S(2)}, u32[]{:S(2)}) collective-permute-start(s32[4]{0:T(128)S(1)} %get-tuple-element.40), channel_id=1, source_target_pairs={{8,0},{12,4},{16,8},{20,12},{24,16},{28,20},{32,24},{36,28},{40,32... | collective-permute-start | bytes 56 | tf_op jit(solution)/shard_map/ppermute | solution.py:14
  56.7 16.8 %collective-permute-start.6 = (s32[4]{0:T(128)S(1)}, s32[4]{0:T(128)S(1)}, u32[]{:S(2)}, u32[]{:S(2)}) collective-permute-start(s32[4]{0:T(128)S(1)} %get-tuple-element.39), channel_id=1, source_target_pairs={{12,0},{16,4},{20,8},{24,12},{28,16},{32,20},{36,24},{40,28},{44,3... | collective-permute-start | bytes 56 | tf_op jit(solution)/shard_map/ppermute | solution.py:14
  58.7 19.7 %collective-permute-start.7 = (s32[4]{0:T(128)S(1)}, s32[4]{0:T(128)S(1)}, u32[]{:S(2)}, u32[]{:S(2)}) collective-permute-start(s32[4]{0:T(128)S(1)} %get-tuple-element.38), channel_id=1, source_target_pairs={{16,0},{20,4},{24,8},{28,12},{32,16},{36,20},{40,24},{44,28},{48,3... | collective-permute-start | bytes 56 | tf_op jit(solution)/shard_map/ppermute | solution.py:14
  63.9 81.7 %collective-permute-start.8 = (f32[4,320]{1,0:T(4,128)S(1)}, f32[4,320]{1,0:T(4,128)S(1)}, u32[]{:S(2)}, u32[]{:S(2)}) collective-permute-start(f32[4,320]{1,0:T(4,128)S(1)} %get-tuple-element.21), channel_id=1, source_target_pairs={{508,0},{0,4},{4,8},{8,12},{12,16},{16,20},{20,24},{24,28},{28,32}... | collective-permute-start | bytes 15368 | tf_op jit(solution)/shard_map/ppermute | solution.py:14
  67.4 81.6 %collective-permute-start.9 = (f32[4,320]{1,0:T(4,128)S(1)}, f32[4,320]{1,0:T(4,128)S(1)}, u32[]{:S(2)}, u32[]{:S(2)}) collective-permute-start(f32[4,320]{1,0:T(4,128)S(1)} %get-tuple-element.20), channel_id=1, source_target_pairs={{504,0},{508,4},{0,8},{4,12},{8,16},{12,20},{16,24},{20,28},{24,32... | collective-permute-start | bytes 15368 | tf_op jit(solution)/shard_map/ppermute | solution.py:14
  69.6 86.2 %collective-permute-start.10 = (f32[4,320]{1,0:T(4,128)S(1)}, f32[4,320]{1,0:T(4,128)S(1)}, u32[]{:S(2)}, u32[]{:S(2)}) collective-permute-start(f32[4,320]{1,0:T(4,128)S(1)} %get-tuple-element.19), channel_id=1, source_target_pairs={{500,0},{504,4},{508,8},{0,12},{4,16},{8,20},{12,24},{16,28},{20,3... | collective-permute-start | bytes 15368 | tf_op jit(solution)/shard_map/ppermute | solution.py:14
  73.6 84.2 %collective-permute-start.11 = (f32[4,320]{1,0:T(4,128)S(1)}, f32[4,320]{1,0:T(4,128)S(1)}, u32[]{:S(2)}, u32[]{:S(2)}) collective-permute-start(f32[4,320]{1,0:T(4,128)S(1)} %get-tuple-element.18), channel_id=1, source_target_pairs={{496,0},{500,4},{504,8},{508,12},{0,16},{4,20},{8,24},{12,28},{16,... | collective-permute-start | bytes 15368 | tf_op jit(solution)/shard_map/ppermute | solution.py:14
  79.3 102.0 %copy-start.3 = (bf16[8,80,320]{2,1,0:T(8,128)(2,1)S(1)}, bf16[8,80,320]{2,1,0:T(8,128)(2,1)}, u32[]{:S(2)}) copy-start(bf16[8,80,320]{2,1,0:T(8,128)(2,1)} %param.15) | copy-start | bytes 1228804
  79.4 3.5 %collective-permute-start.16 = (bf16[4,320]{1,0:T(4,128)(2,1)S(1)}, bf16[4,320]{1,0:T(4,128)(2,1)S(1)}, u32[]{:S(2)}, u32[]{:S(2)}) collective-permute-start(bf16[4,320]{1,0:T(4,128)(2,1)S(1)} %get-tuple-element.37), channel_id=1, source_target_pairs={{4,0},{8,4},{12,8},{16,12},{20,16},{24,20},{28,24},{32,28},{36,32}... | collective-permute-start | bytes 7688 | tf_op jit(solution)/shard_map/ppermute | solution.py:14
  82.8 5.6 %collective-permute-start.17 = (bf16[4,320]{1,0:T(4,128)(2,1)S(1)}, bf16[4,320]{1,0:T(4,128)(2,1)S(1)}, u32[]{:S(2)}, u32[]{:S(2)}) collective-permute-start(bf16[4,320]{1,0:T(4,128)(2,1)S(1)} %get-tuple-element.36), channel_id=1, source_target_pairs={{8,0},{12,4},{16,8},{20,12},{24,16},{28,20},{32,24},{36,28},{40,32... | collective-permute-start | bytes 7688 | tf_op jit(solution)/shard_map/ppermute | solution.py:14
  88.4 9.4 %collective-permute-start.18 = (bf16[4,320]{1,0:T(4,128)(2,1)S(1)}, bf16[4,320]{1,0:T(4,128)(2,1)S(1)}, u32[]{:S(2)}, u32[]{:S(2)}) collective-permute-start(bf16[4,320]{1,0:T(4,128)(2,1)S(1)} %get-tuple-element.35), channel_id=1, source_target_pairs={{12,0},{16,4},{20,8},{24,12},{28,16},{32,20},{36,24},{40,28},{44,3... | collective-permute-start | bytes 7688 | tf_op jit(solution)/shard_map/ppermute | solution.py:14
  97.8 7.6 %collective-permute-start.19 = (bf16[4,320]{1,0:T(4,128)(2,1)S(1)}, bf16[4,320]{1,0:T(4,128)(2,1)S(1)}, u32[]{:S(2)}, u32[]{:S(2)}) collective-permute-start(bf16[4,320]{1,0:T(4,128)(2,1)S(1)} %get-tuple-element.34), channel_id=1, source_target_pairs={{16,0},{20,4},{24,8},{28,12},{32,16},{36,20},{40,24},{44,28},{48,3... | collective-permute-start | bytes 7688 | tf_op jit(solution)/shard_map/ppermute | solution.py:14
  105.4 9.2 %collective-permute-start.20 = (bf16[4,320]{1,0:T(4,128)(2,1)S(1)}, bf16[4,320]{1,0:T(4,128)(2,1)S(1)}, u32[]{:S(2)}, u32[]{:S(2)}) collective-permute-start(bf16[4,320]{1,0:T(4,128)(2,1)S(1)} %get-tuple-element.33), channel_id=1, source_target_pairs={{508,0},{0,4},{4,8},{8,12},{12,16},{16,20},{20,24},{24,28},{28,32}... | collective-permute-start | bytes 7688 | tf_op jit(solution)/shard_map/ppermute | solution.py:14
  114.6 5.5 %collective-permute-start.21 = (bf16[4,320]{1,0:T(4,128)(2,1)S(1)}, bf16[4,320]{1,0:T(4,128)(2,1)S(1)}, u32[]{:S(2)}, u32[]{:S(2)}) collective-permute-start(bf16[4,320]{1,0:T(4,128)(2,1)S(1)} %get-tuple-element.32), channel_id=1, source_target_pairs={{504,0},{508,4},{0,8},{4,12},{8,16},{12,20},{16,24},{20,28},{24,32... | collective-permute-start | bytes 7688 | tf_op jit(solution)/shard_map/ppermute | solution.py:14
  120.1 6.4 %collective-permute-start.22 = (bf16[4,320]{1,0:T(4,128)(2,1)S(1)}, bf16[4,320]{1,0:T(4,128)(2,1)S(1)}, u32[]{:S(2)}, u32[]{:S(2)}) collective-permute-start(bf16[4,320]{1,0:T(4,128)(2,1)S(1)} %get-tuple-element.31), channel_id=1, source_target_pairs={{500,0},{504,4},{508,8},{0,12},{4,16},{8,20},{12,24},{16,28},{20,3... | collective-permute-start | bytes 7688 | tf_op jit(solution)/shard_map/ppermute | solution.py:14
  126.4 15.7 %collective-permute-start.23 = (bf16[4,320]{1,0:T(4,128)(2,1)S(1)}, bf16[4,320]{1,0:T(4,128)(2,1)S(1)}, u32[]{:S(2)}, u32[]{:S(2)}) collective-permute-start(bf16[4,320]{1,0:T(4,128)(2,1)S(1)} %get-tuple-element.30), channel_id=1, source_target_pairs={{496,0},{500,4},{504,8},{508,12},{0,16},{4,20},{8,24},{12,28},{16,... | collective-permute-start | bytes 7688 | tf_op jit(solution)/shard_map/ppermute | solution.py:14
  142.2 15.6 %collective-permute-start.12 = (f32[4,320]{1,0:T(4,128)S(1)}, f32[4,320]{1,0:T(4,128)S(1)}, u32[]{:S(2)}, u32[]{:S(2)}) collective-permute-start(f32[4,320]{1,0:T(4,128)S(1)} %get-tuple-element.17), channel_id=1, source_target_pairs={{4,0},{8,4},{12,8},{16,12},{20,16},{24,20},{28,24},{32,28},{36,32}... | collective-permute-start | bytes 15368 | tf_op jit(solution)/shard_map/ppermute | solution.py:14
  144.8 36.7 %copy-start.1 = (f32[8,80]{1,0:T(8,128)S(1)}, f32[8,80]{1,0:T(8,128)}, u32[]{:S(2)}) copy-start(f32[8,80]{1,0:T(8,128)} %param.14) | copy-start | bytes 7684
  145.6 12.2 %collective-permute-start.13 = (f32[4,320]{1,0:T(4,128)S(1)}, f32[4,320]{1,0:T(4,128)S(1)}, u32[]{:S(2)}, u32[]{:S(2)}) collective-permute-start(f32[4,320]{1,0:T(4,128)S(1)} %get-tuple-element.16), channel_id=1, source_target_pairs={{8,0},{12,4},{16,8},{20,12},{24,16},{28,20},{32,24},{36,28},{40,32... | collective-permute-start | bytes 15368 | tf_op jit(solution)/shard_map/ppermute | solution.py:14
  149.0 8.8 %collective-permute-start.14 = (f32[4,320]{1,0:T(4,128)S(1)}, f32[4,320]{1,0:T(4,128)S(1)}, u32[]{:S(2)}, u32[]{:S(2)}) collective-permute-start(f32[4,320]{1,0:T(4,128)S(1)} %get-tuple-element.15), channel_id=1, source_target_pairs={{12,0},{16,4},{20,8},{24,12},{28,16},{32,20},{36,24},{40,28},{44,3... | collective-permute-start | bytes 15368 | tf_op jit(solution)/shard_map/ppermute | solution.py:14
  155.9 7.6 %collective-permute-start.15 = (f32[4,320]{1,0:T(4,128)S(1)}, f32[4,320]{1,0:T(4,128)S(1)}, u32[]{:S(2)}, u32[]{:S(2)}) collective-permute-start(f32[4,320]{1,0:T(4,128)S(1)} %get-tuple-element.14), channel_id=1, source_target_pairs={{16,0},{20,4},{24,8},{28,12},{32,16},{36,20},{40,24},{44,28},{48,3... | collective-permute-start | bytes 15368 | tf_op jit(solution)/shard_map/ppermute | solution.py:14
  194.6 13.3 %collective-permute-start.32 = (bf16[4,320]{1,0:T(4,128)(2,1)S(1)}, bf16[4,320]{1,0:T(4,128)(2,1)S(1)}, u32[]{:S(2)}, u32[]{:S(2)}) collective-permute-start(bf16[4,320]{1,0:T(4,128)(2,1)S(1)} %get-tuple-element.29), channel_id=1, source_target_pairs={{4,0},{8,4},{12,8},{16,12},{20,16},{24,20},{28,24},{32,28},{36,32}... | collective-permute-start | bytes 7688 | tf_op jit(solution)/shard_map/ppermute | solution.py:14
  198.0 70.4 %collective-permute-start.24 = (f32[4,320]{1,0:T(4,128)S(1)}, f32[4,320]{1,0:T(4,128)S(1)}, u32[]{:S(2)}, u32[]{:S(2)}) collective-permute-start(f32[4,320]{1,0:T(4,128)S(1)} %get-tuple-element.13), channel_id=1, source_target_pairs={{508,0},{0,4},{4,8},{8,12},{12,16},{16,20},{20,24},{24,28},{28,32}... | collective-permute-start | bytes 15368 | tf_op jit(solution)/shard_map/ppermute | solution.py:14
  200.5 71.4 %collective-permute-start.25 = (f32[4,320]{1,0:T(4,128)S(1)}, f32[4,320]{1,0:T(4,128)S(1)}, u32[]{:S(2)}, u32[]{:S(2)}) collective-permute-start(f32[4,320]{1,0:T(4,128)S(1)} %get-tuple-element.12), channel_id=1, source_target_pairs={{504,0},{508,4},{0,8},{4,12},{8,16},{12,20},{16,24},{20,28},{24,32... | collective-permute-start | bytes 15368 | tf_op jit(solution)/shard_map/ppermute | solution.py:14
  204.1 74.6 %collective-permute-start.26 = (f32[4,320]{1,0:T(4,128)S(1)}, f32[4,320]{1,0:T(4,128)S(1)}, u32[]{:S(2)}, u32[]{:S(2)}) collective-permute-start(f32[4,320]{1,0:T(4,128)S(1)} %get-tuple-element.11), channel_id=1, source_target_pairs={{500,0},{504,4},{508,8},{0,12},{4,16},{8,20},{12,24},{16,28},{20,3... | collective-permute-start | bytes 15368 | tf_op jit(solution)/shard_map/ppermute | solution.py:14
  206.0 74.6 %collective-permute-start.27 = (f32[4,320]{1,0:T(4,128)S(1)}, f32[4,320]{1,0:T(4,128)S(1)}, u32[]{:S(2)}, u32[]{:S(2)}) collective-permute-start(f32[4,320]{1,0:T(4,128)S(1)} %get-tuple-element.10), channel_id=1, source_target_pairs={{496,0},{500,4},{504,8},{508,12},{0,16},{4,20},{8,24},{12,28},{16,... | collective-permute-start | bytes 15368 | tf_op jit(solution)/shard_map/ppermute | solution.py:14
  208.0 5.5 %collective-permute-start.33 = (bf16[4,320]{1,0:T(4,128)(2,1)S(1)}, bf16[4,320]{1,0:T(4,128)(2,1)S(1)}, u32[]{:S(2)}, u32[]{:S(2)}) collective-permute-start(bf16[4,320]{1,0:T(4,128)(2,1)S(1)} %get-tuple-element.28), channel_id=1, source_target_pairs={{8,0},{12,4},{16,8},{20,12},{24,16},{28,20},{32,24},{36,28},{40,32... | collective-permute-start | bytes 7688 | tf_op jit(solution)/shard_map/ppermute | solution.py:14
  213.5 7.2 %collective-permute-start.34 = (bf16[4,320]{1,0:T(4,128)(2,1)S(1)}, bf16[4,320]{1,0:T(4,128)(2,1)S(1)}, u32[]{:S(2)}, u32[]{:S(2)}) collective-permute-start(bf16[4,320]{1,0:T(4,128)(2,1)S(1)} %get-tuple-element.27), channel_id=1, source_target_pairs={{12,0},{16,4},{20,8},{24,12},{28,16},{32,20},{36,24},{40,28},{44,3... | collective-permute-start | bytes 7688 | tf_op jit(solution)/shard_map/ppermute | solution.py:14
  220.7 7.6 %collective-permute-start.35 = (bf16[4,320]{1,0:T(4,128)(2,1)S(1)}, bf16[4,320]{1,0:T(4,128)(2,1)S(1)}, u32[]{:S(2)}, u32[]{:S(2)}) collective-permute-start(bf16[4,320]{1,0:T(4,128)(2,1)S(1)} %get-tuple-element.26), channel_id=1, source_target_pairs={{16,0},{20,4},{24,8},{28,12},{32,16},{36,20},{40,24},{44,28},{48,3... | collective-permute-start | bytes 7688 | tf_op jit(solution)/shard_map/ppermute | solution.py:14
  228.3 9.2 %collective-permute-start.36 = (bf16[4,320]{1,0:T(4,128)(2,1)S(1)}, bf16[4,320]{1,0:T(4,128)(2,1)S(1)}, u32[]{:S(2)}, u32[]{:S(2)}) collective-permute-start(bf16[4,320]{1,0:T(4,128)(2,1)S(1)} %get-tuple-element.25), channel_id=1, source_target_pairs={{508,0},{0,4},{4,8},{8,12},{12,16},{16,20},{20,24},{24,28},{28,32}... | collective-permute-start | bytes 7688 | tf_op jit(solution)/shard_map/ppermute | solution.py:14
  237.4 6.8 %collective-permute-start.37 = (bf16[4,320]{1,0:T(4,128)(2,1)S(1)}, bf16[4,320]{1,0:T(4,128)(2,1)S(1)}, u32[]{:S(2)}, u32[]{:S(2)}) collective-permute-start(bf16[4,320]{1,0:T(4,128)(2,1)S(1)} %get-tuple-element.24), channel_id=1, source_target_pairs={{504,0},{508,4},{0,8},{4,12},{8,16},{12,20},{16,24},{20,28},{24,32... | collective-permute-start | bytes 7688 | tf_op jit(solution)/shard_map/ppermute | solution.py:14
  244.2 6.6 %collective-permute-start.38 = (bf16[4,320]{1,0:T(4,128)(2,1)S(1)}, bf16[4,320]{1,0:T(4,128)(2,1)S(1)}, u32[]{:S(2)}, u32[]{:S(2)}) collective-permute-start(bf16[4,320]{1,0:T(4,128)(2,1)S(1)} %get-tuple-element.23), channel_id=1, source_target_pairs={{500,0},{504,4},{508,8},{0,12},{4,16},{8,20},{12,24},{16,28},{20,3... | collective-permute-start | bytes 7688 | tf_op jit(solution)/shard_map/ppermute | solution.py:14
  250.7 14.3 %collective-permute-start.39 = (bf16[4,320]{1,0:T(4,128)(2,1)S(1)}, bf16[4,320]{1,0:T(4,128)(2,1)S(1)}, u32[]{:S(2)}, u32[]{:S(2)}) collective-permute-start(bf16[4,320]{1,0:T(4,128)(2,1)S(1)} %get-tuple-element.22), channel_id=1, source_target_pairs={{496,0},{500,4},{504,8},{508,12},{0,16},{4,20},{8,24},{12,28},{16,... | collective-permute-start | bytes 7688 | tf_op jit(solution)/shard_map/ppermute | solution.py:14
  265.0 15.6 %collective-permute-start.28 = (f32[4,320]{1,0:T(4,128)S(1)}, f32[4,320]{1,0:T(4,128)S(1)}, u32[]{:S(2)}, u32[]{:S(2)}) collective-permute-start(f32[4,320]{1,0:T(4,128)S(1)} %get-tuple-element.9), channel_id=1, source_target_pairs={{4,0},{8,4},{12,8},{16,12},{20,16},{24,20},{28,24},{32,28},{36,32}... | collective-permute-start | bytes 15368 | tf_op jit(solution)/shard_map/ppermute | solution.py:14
  267.7 35.2 %copy-start.2 = (f32[8,80]{1,0:T(8,128)S(1)}, f32[8,80]{1,0:T(8,128)}, u32[]{:S(2)}) copy-start(f32[8,80]{1,0:T(8,128)} %param.17) | copy-start | bytes 7684
  268.4 12.2 %collective-permute-start.29 = (f32[4,320]{1,0:T(4,128)S(1)}, f32[4,320]{1,0:T(4,128)S(1)}, u32[]{:S(2)}, u32[]{:S(2)}) collective-permute-start(f32[4,320]{1,0:T(4,128)S(1)} %get-tuple-element.8), channel_id=1, source_target_pairs={{8,0},{12,4},{16,8},{20,12},{24,16},{28,20},{32,24},{36,28},{40,32... | collective-permute-start | bytes 15368 | tf_op jit(solution)/shard_map/ppermute | solution.py:14
  271.9 8.8 %collective-permute-start.30 = (f32[4,320]{1,0:T(4,128)S(1)}, f32[4,320]{1,0:T(4,128)S(1)}, u32[]{:S(2)}, u32[]{:S(2)}) collective-permute-start(f32[4,320]{1,0:T(4,128)S(1)} %get-tuple-element.7), channel_id=1, source_target_pairs={{12,0},{16,4},{20,8},{24,12},{28,16},{32,20},{36,24},{40,28},{44,3... | collective-permute-start | bytes 15368 | tf_op jit(solution)/shard_map/ppermute | solution.py:14
  278.7 7.6 %collective-permute-start.31 = (f32[4,320]{1,0:T(4,128)S(1)}, f32[4,320]{1,0:T(4,128)S(1)}, u32[]{:S(2)}, u32[]{:S(2)}) collective-permute-start(f32[4,320]{1,0:T(4,128)S(1)} %get-tuple-element.6), channel_id=1, source_target_pairs={{16,0},{20,4},{24,8},{28,12},{32,16},{36,20},{40,24},{44,28},{48,3... | collective-permute-start | bytes 15368 | tf_op jit(solution)/shard_map/ppermute | solution.py:14
where the time goes:
time: 315 us; the launch traced here: 313 us
  starting transfers between devices  130 us (41%)
  waiting for transfers between devices  83.1 us (26%)
  blocking collectives  71.8 us (23%)
  other arithmetic  13.5 us (4%)
  local copies, waits for them, and re-layouts  8.94 us (3%)
  matrix products  4.21 us (1%)
    ppermute x40, starting transfers between devices, from_behind(): return lax.ppermute(block, axis, route)  130 us
    ppermute x40, waiting for transfers between devices, from_behind(): return lax.ppermute(block, axis, route)  83.1 us
    all_gather x3, blocking collectives, full_rows(): return lax.all_gather(values, 'blk', axis=1, tiled=True)  32.2 us
    psum x2, blocking collectives, local(): summed = lax.psum(partial_value, 'blk')  30.1 us
    psum x1, blocking collectives, local(): indicator = lax.psum(weights, 'blk')  9.47 us
  transfers between devices with their start and end apart: 40, of which 17 were waited for; matrix products, arithmetic and copies ran while one was open for 5% of the time, Pallas kernels for 0%

commit v1 on v0

--- a/solution.py
+++ b/solution.py
@@ -15,7 +15,9 @@
 
 
 def full_rows(values):
-    return lax.all_gather(values, "blk", axis=1, tiled=True)
+    return jnp.concatenate(
+        lax.all_to_all(jnp.stack([values] * lax.axis_size("blk")), "blk", 0, 0), axis=1
+    )
 
 
 def local(degree, face_elem, face_side, face_peer, coupling, inv_diag, inv_off, source, residual):

time: 315 us -> 237 us (0.75)
  the two profiles are of different devices: /device:TPU:64 before, /device:TPU:40 now
where the time goes in v1:
time: 237 us; the launch traced here: 236 us
  starting transfers between devices  151 us (64%)
  blocking collectives  39.4 us (17%)
  waiting for transfers between devices  15.4 us (6%)
  other arithmetic  12.9 us (5%)
  local copies, waits for them, and re-layouts  10.9 us (5%)
  matrix products  4.21 us (2%)
    ppermute x40, starting transfers between devices, from_behind(): return lax.ppermute(block, axis, route)  135 us
    psum x2, blocking collectives, local(): summed = lax.psum(partial_value, 'blk')  27.7 us
    all_to_all x3, starting transfers between devices, full_rows(): lax.all_to_all(jnp.stack([values] * lax.axis_size('blk')), 'blk', 0, 0)  16.4 us
    ppermute x40, waiting for transfers between devices, from_behind(): return lax.ppermute(block, axis, route)  15.4 us
    psum x1, blocking collectives, local(): indicator = lax.psum(weights, 'blk')  11.7 us
  transfers between devices with their start and end apart: 43, of which 5 were waited for; matrix products, arithmetic and copies ran while one was open for 6% of the time, Pallas kernels for 0%

profile of v1, /device:TPU:40, one launch (start us, length us, event | category | flops | bytes accessed | tf_op | source)
XLA Modules:
  0.0 235.8 jit_solution(13294777938324677013)
XLA Ops:
  2.9 4.9 %all-to-all-start = ((bf16[4,8,80]{2,1,0:T(8,128)(2,1)}), bf16[4,8,80]{2,1,0:T(8,128)(2,1)S(1)}, u32[]{:S(2)}, u32[]{:S(2)}) async-start(bf16[4,8,80]{2,1,0:T(8,128)(2,1)} %stack.174), calls=%async_computation | async-start | bytes 16384 | tf_op jit(solution)/shard_map/all_to_all | solution.py:19
  12.9 3.8 %collective-permute-start.1 = (s32[4]{0:T(128)S(1)}, s32[4]{0:T(128)S(1)}, u32[]{:S(2)}, u32[]{:S(2)}) collective-permute-start(s32[4]{0:T(128)S(1)} %get-tuple-element.44), channel_id=1, source_target_pairs={{504,0},{508,4},{0,8},{4,12},{8,16},{12,20},{16,24},{20,28},{24,32... | collective-permute-start | bytes 56 | tf_op jit(solution)/shard_map/ppermute | solution.py:14
  16.8 6.4 %collective-permute-start.2 = (s32[4]{0:T(128)S(1)}, s32[4]{0:T(128)S(1)}, u32[]{:S(2)}, u32[]{:S(2)}) collective-permute-start(s32[4]{0:T(128)S(1)} %get-tuple-element.43), channel_id=1, source_target_pairs={{500,0},{504,4},{508,8},{0,12},{4,16},{8,20},{12,24},{16,28},{20,3... | collective-permute-start | bytes 56 | tf_op jit(solution)/shard_map/ppermute | solution.py:14
  23.2 5.2 %collective-permute-start.3 = (s32[4]{0:T(128)S(1)}, s32[4]{0:T(128)S(1)}, u32[]{:S(2)}, u32[]{:S(2)}) collective-permute-start(s32[4]{0:T(128)S(1)} %get-tuple-element.42), channel_id=1, source_target_pairs={{496,0},{500,4},{504,8},{508,12},{0,16},{4,20},{8,24},{12,28},{16,... | collective-permute-start | bytes 56 | tf_op jit(solution)/shard_map/ppermute | solution.py:14
  28.3 1.9 collective-permute-start.4
  32.3 4.9 %collective-permute-start.5 = (s32[4]{0:T(128)S(1)}, s32[4]{0:T(128)S(1)}, u32[]{:S(2)}, u32[]{:S(2)}) collective-permute-start(s32[4]{0:T(128)S(1)} %get-tuple-element.40), channel_id=1, source_target_pairs={{8,0},{12,4},{16,8},{20,12},{24,16},{28,20},{32,24},{36,28},{40,32... | collective-permute-start | bytes 56 | tf_op jit(solution)/shard_map/ppermute | solution.py:14
  37.2 2.4 %collective-permute-start.6 = (s32[4]{0:T(128)S(1)}, s32[4]{0:T(128)S(1)}, u32[]{:S(2)}, u32[]{:S(2)}) collective-permute-start(s32[4]{0:T(128)S(1)} %get-tuple-element.39), channel_id=1, source_target_pairs={{12,0},{16,4},{20,8},{24,12},{28,16},{32,20},{36,24},{40,28},{44,3... | collective-permute-start | bytes 56 | tf_op jit(solution)/shard_map/ppermute | solution.py:14
  39.6 4.8 %collective-permute-start.7 = (s32[4]{0:T(128)S(1)}, s32[4]{0:T(128)S(1)}, u32[]{:S(2)}, u32[]{:S(2)}) collective-permute-start(s32[4]{0:T(128)S(1)} %get-tuple-element.38), channel_id=1, source_target_pairs={{16,0},{20,4},{24,8},{28,12},{32,16},{36,20},{40,24},{44,28},{48,3... | collective-permute-start | bytes 56 | tf_op jit(solution)/shard_map/ppermute | solution.py:14
  49.8 4.8 %all-to-all-start.1 = ((bf16[4,8,80]{2,1,0:T(8,128)(2,1)}), bf16[4,8,80]{2,1,0:T(8,128)(2,1)S(1)}, u32[]{:S(2)}, u32[]{:S(2)}) async-start(bf16[4,8,80]{2,1,0:T(8,128)(2,1)} %stack.193), calls=%async_computation.1 | async-start | bytes 16384 | tf_op jit(solution)/shard_map/all_to_all | solution.py:19
  56.6 1.9 collective-permute-start.8
  58.5 4.5 %collective-permute-start.9 = (f32[4,320]{1,0:T(4,128)S(1)}, f32[4,320]{1,0:T(4,128)S(1)}, u32[]{:S(2)}, u32[]{:S(2)}) collective-permute-start(f32[4,320]{1,0:T(4,128)S(1)} %get-tuple-element.20), channel_id=1, source_target_pairs={{504,0},{508,4},{0,8},{4,12},{8,16},{12,20},{16,24},{20,28},{24,32... | collective-permute-start | bytes 15368 | tf_op jit(solution)/shard_map/ppermute | solution.py:14
  63.0 3.6 %collective-permute-start.10 = (f32[4,320]{1,0:T(4,128)S(1)}, f32[4,320]{1,0:T(4,128)S(1)}, u32[]{:S(2)}, u32[]{:S(2)}) collective-permute-start(f32[4,320]{1,0:T(4,128)S(1)} %get-tuple-element.19), channel_id=1, source_target_pairs={{500,0},{504,4},{508,8},{0,12},{4,16},{8,20},{12,24},{16,28},{20,3... | collective-permute-start | bytes 15368 | tf_op jit(solution)/shard_map/ppermute | solution.py:14
  66.6 5.9 %collective-permute-start.11 = (f32[4,320]{1,0:T(4,128)S(1)}, f32[4,320]{1,0:T(4,128)S(1)}, u32[]{:S(2)}, u32[]{:S(2)}) collective-permute-start(f32[4,320]{1,0:T(4,128)S(1)} %get-tuple-element.18), channel_id=1, source_target_pairs={{496,0},{500,4},{504,8},{508,12},{0,16},{4,20},{8,24},{12,28},{16,... | collective-permute-start | bytes 15368 | tf_op jit(solution)/shard_map/ppermute | solution.py:14
  72.5 1.9 collective-permute-start.12
  75.8 4.3 %collective-permute-start.13 = (f32[4,320]{1,0:T(4,128)S(1)}, f32[4,320]{1,0:T(4,128)S(1)}, u32[]{:S(2)}, u32[]{:S(2)}) collective-permute-start(f32[4,320]{1,0:T(4,128)S(1)} %get-tuple-element.16), channel_id=1, source_target_pairs={{8,0},{12,4},{16,8},{20,12},{24,16},{28,20},{32,24},{36,28},{40,32... | collective-permute-start | bytes 15368 | tf_op jit(solution)/shard_map/ppermute | solution.py:14
  80.2 2.0 collective-permute-start.14
  82.2 3.5 %collective-permute-start.15 = (f32[4,320]{1,0:T(4,128)S(1)}, f32[4,320]{1,0:T(4,128)S(1)}, u32[]{:S(2)}, u32[]{:S(2)}) collective-permute-start(f32[4,320]{1,0:T(4,128)S(1)} %get-tuple-element.14), channel_id=1, source_target_pairs={{16,0},{20,4},{24,8},{28,12},{32,16},{36,20},{40,24},{44,28},{48,3... | collective-permute-start | bytes 15368 | tf_op jit(solution)/shard_map/ppermute | solution.py:14
  85.8 4.7 %collective-permute-start.16 = (bf16[4,320]{1,0:T(4,128)(2,1)S(1)}, bf16[4,320]{1,0:T(4,128)(2,1)S(1)}, u32[]{:S(2)}, u32[]{:S(2)}) collective-permute-start(bf16[4,320]{1,0:T(4,128)(2,1)S(1)} %get-tuple-element.37), channel_id=1, source_target_pairs={{4,0},{8,4},{12,8},{16,12},{20,16},{24,20},{28,24},{32,28},{36,32}... | collective-permute-start | bytes 7688 | tf_op jit(solution)/shard_map/ppermute | solution.py:14
  90.5 3.4 %collective-permute-start.17 = (bf16[4,320]{1,0:T(4,128)(2,1)S(1)}, bf16[4,320]{1,0:T(4,128)(2,1)S(1)}, u32[]{:S(2)}, u32[]{:S(2)}) collective-permute-start(bf16[4,320]{1,0:T(4,128)(2,1)S(1)} %get-tuple-element.36), channel_id=1, source_target_pairs={{8,0},{12,4},{16,8},{20,12},{24,16},{28,20},{32,24},{36,28},{40,32... | collective-permute-start | bytes 7688 | tf_op jit(solution)/shard_map/ppermute | solution.py:14
  93.9 3.3 %collective-permute-start.18 = (bf16[4,320]{1,0:T(4,128)(2,1)S(1)}, bf16[4,320]{1,0:T(4,128)(2,1)S(1)}, u32[]{:S(2)}, u32[]{:S(2)}) collective-permute-start(bf16[4,320]{1,0:T(4,128)(2,1)S(1)} %get-tuple-element.35), channel_id=1, source_target_pairs={{12,0},{16,4},{20,8},{24,12},{28,16},{32,20},{36,24},{40,28},{44,3... | collective-permute-start | bytes 7688 | tf_op jit(solution)/shard_map/ppermute | solution.py:14
  97.3 2.3 collective-permute-start.19
  99.6 2.0 collective-permute-start.20
  102.5 3.6 %collective-permute-start.21 = (bf16[4,320]{1,0:T(4,128)(2,1)S(1)}, bf16[4,320]{1,0:T(4,128)(2,1)S(1)}, u32[]{:S(2)}, u32[]{:S(2)}) collective-permute-start(bf16[4,320]{1,0:T(4,128)(2,1)S(1)} %get-tuple-element.32), channel_id=1, source_target_pairs={{504,0},{508,4},{0,8},{4,12},{8,16},{12,20},{16,24},{20,28},{24,32... | collective-permute-start | bytes 7688 | tf_op jit(solution)/shard_map/ppermute | solution.py:14
  106.2 4.1 %collective-permute-start.22 = (bf16[4,320]{1,0:T(4,128)(2,1)S(1)}, bf16[4,320]{1,0:T(4,128)(2,1)S(1)}, u32[]{:S(2)}, u32[]{:S(2)}) collective-permute-start(bf16[4,320]{1,0:T(4,128)(2,1)S(1)} %get-tuple-element.31), channel_id=1, source_target_pairs={{500,0},{504,4},{508,8},{0,12},{4,16},{8,20},{12,24},{16,28},{20,3... | collective-permute-start | bytes 7688 | tf_op jit(solution)/shard_map/ppermute | solution.py:14
  110.4 2.1 collective-permute-start.23
  112.5 2.8 %collective-permute-done.22 = bf16[4,320]{1,0:T(4,128)(2,1)S(1)} collective-permute-done((bf16[4,320]{1,0:T(4,128)(2,1)S(1)}, bf16[4,320]{1,0:T(4,128)(2,1)S(1)}, u32[]{:S(2)}, u32[]{:S(2)}) %collective-permute-start.22) | collective-permute-done | bytes 2592 | tf_op jit(solution)/shard_map/ppermute | solution.py:14
  115.3 4.7 %collective-permute-done.23 = bf16[4,320]{1,0:T(4,128)(2,1)S(1)} collective-permute-done((bf16[4,320]{1,0:T(4,128)(2,1)S(1)}, bf16[4,320]{1,0:T(4,128)(2,1)S(1)}, u32[]{:S(2)}, u32[]{:S(2)}) %collective-permute-start.23) | collective-permute-done | bytes 2592 | tf_op jit(solution)/shard_map/ppermute | solution.py:14
  122.6 13.8 %psum.21 = bf16[8,320]{1,0:T(8,128)(2,1)S(1)} all-reduce(f32[8,320]{1,0:T(8,128)S(1)} %dynamic_update_slice.6), channel_id=1, replica_groups=mesh['dom'=128,'blk'=4] {'blk'}, use_global_device_ids=true, to_apply=%region_7.8 | all-reduce | flops 2560 | bytes 15360 | tf_op jit(solution)/shard_map/psum | solution.py:100
  139.4 6.7 %all-to-all-start.2 = ((bf16[4,8,80]{2,1,0:T(8,128)(2,1)}), bf16[4,8,80]{2,1,0:T(8,128)(2,1)S(1)}, u32[]{:S(2)}, u32[]{:S(2)}) async-start(bf16[4,8,80]{2,1,0:T(8,128)(2,1)} %stack.221), calls=%async_computation.2 | async-start | bytes 16384 | tf_op jit(solution)/shard_map/all_to_all | solution.py:19
  146.9 1.9 collective-permute-start.24
  148.8 1.9 collective-permute-start.25
  150.7 1.9 collective-permute-start.26
  152.7 1.9 collective-permute-start.27
  154.6 3.6 %collective-permute-start.28 = (f32[4,320]{1,0:T(4,128)S(1)}, f32[4,320]{1,0:T(4,128)S(1)}, u32[]{:S(2)}, u32[]{:S(2)}) collective-permute-start(f32[4,320]{1,0:T(4,128)S(1)} %get-tuple-element.9), channel_id=1, source_target_pairs={{4,0},{8,4},{12,8},{16,12},{20,16},{24,20},{28,24},{32,28},{36,32}... | collective-permute-start | bytes 15368 | tf_op jit(solution)/shard_map/ppermute | solution.py:14
  159.6 7.0 %collective-permute-start.29 = (f32[4,320]{1,0:T(4,128)S(1)}, f32[4,320]{1,0:T(4,128)S(1)}, u32[]{:S(2)}, u32[]{:S(2)}) collective-permute-start(f32[4,320]{1,0:T(4,128)S(1)} %get-tuple-element.8), channel_id=1, source_target_pairs={{8,0},{12,4},{16,8},{20,12},{24,16},{28,20},{32,24},{36,28},{40,32... | collective-permute-start | bytes 15368 | tf_op jit(solution)/shard_map/ppermute | solution.py:14
  166.6 3.2 %collective-permute-start.30 = (f32[4,320]{1,0:T(4,128)S(1)}, f32[4,320]{1,0:T(4,128)S(1)}, u32[]{:S(2)}, u32[]{:S(2)}) collective-permute-start(f32[4,320]{1,0:T(4,128)S(1)} %get-tuple-element.7), channel_id=1, source_target_pairs={{12,0},{16,4},{20,8},{24,12},{28,16},{32,20},{36,24},{40,28},{44,3... | collective-permute-start | bytes 15368 | tf_op jit(solution)/shard_map/ppermute | solution.py:14
  169.9 4.8 %collective-permute-start.31 = (f32[4,320]{1,0:T(4,128)S(1)}, f32[4,320]{1,0:T(4,128)S(1)}, u32[]{:S(2)}, u32[]{:S(2)}) collective-permute-start(f32[4,320]{1,0:T(4,128)S(1)} %get-tuple-element.6), channel_id=1, source_target_pairs={{16,0},{20,4},{24,8},{28,12},{32,16},{36,20},{40,24},{44,28},{48,3... | collective-permute-start | bytes 15368 | tf_op jit(solution)/shard_map/ppermute | solution.py:14
  174.7 3.3 %collective-permute-start.32 = (bf16[4,320]{1,0:T(4,128)(2,1)S(1)}, bf16[4,320]{1,0:T(4,128)(2,1)S(1)}, u32[]{:S(2)}, u32[]{:S(2)}) collective-permute-start(bf16[4,320]{1,0:T(4,128)(2,1)S(1)} %get-tuple-element.29), channel_id=1, source_target_pairs={{4,0},{8,4},{12,8},{16,12},{20,16},{24,20},{28,24},{32,28},{36,32}... | collective-permute-start | bytes 7688 | tf_op jit(solution)/shard_map/ppermute | solution.py:14
  178.0 2.5 %collective-permute-start.33 = (bf16[4,320]{1,0:T(4,128)(2,1)S(1)}, bf16[4,320]{1,0:T(4,128)(2,1)S(1)}, u32[]{:S(2)}, u32[]{:S(2)}) collective-permute-start(bf16[4,320]{1,0:T(4,128)(2,1)S(1)} %get-tuple-element.28), channel_id=1, source_target_pairs={{8,0},{12,4},{16,8},{20,12},{24,16},{28,20},{32,24},{36,28},{40,32... | collective-permute-start | bytes 7688 | tf_op jit(solution)/shard_map/ppermute | solution.py:14
  180.5 1.9 collective-permute-start.34
  182.5 2.2 collective-permute-start.35
  184.7 2.0 collective-permute-start.36
  187.7 3.6 %collective-permute-start.37 = (bf16[4,320]{1,0:T(4,128)(2,1)S(1)}, bf16[4,320]{1,0:T(4,128)(2,1)S(1)}, u32[]{:S(2)}, u32[]{:S(2)}) collective-permute-start(bf16[4,320]{1,0:T(4,128)(2,1)S(1)} %get-tuple-element.24), channel_id=1, source_target_pairs={{504,0},{508,4},{0,8},{4,12},{8,16},{12,20},{16,24},{20,28},{24,32... | collective-permute-start | bytes 7688 | tf_op jit(solution)/shard_map/ppermute | solution.py:14
  191.3 5.4 %collective-permute-start.38 = (bf16[4,320]{1,0:T(4,128)(2,1)S(1)}, bf16[4,320]{1,0:T(4,128)(2,1)S(1)}, u32[]{:S(2)}, u32[]{:S(2)}) collective-permute-start(bf16[4,320]{1,0:T(4,128)(2,1)S(1)} %get-tuple-element.23), channel_id=1, source_target_pairs={{500,0},{504,4},{508,8},{0,12},{4,16},{8,20},{12,24},{16,28},{20,3... | collective-permute-start | bytes 7688 | tf_op jit(solution)/shard_map/ppermute | solution.py:14
  196.7 3.3 %collective-permute-start.39 = (bf16[4,320]{1,0:T(4,128)(2,1)S(1)}, bf16[4,320]{1,0:T(4,128)(2,1)S(1)}, u32[]{:S(2)}, u32[]{:S(2)}) collective-permute-start(bf16[4,320]{1,0:T(4,128)(2,1)S(1)} %get-tuple-element.22), channel_id=1, source_target_pairs={{496,0},{500,4},{504,8},{508,12},{0,16},{4,20},{8,24},{12,28},{16,... | collective-permute-start | bytes 7688 | tf_op jit(solution)/shard_map/ppermute | solution.py:14
  200.5 6.0 %collective-permute-done.39 = bf16[4,320]{1,0:T(4,128)(2,1)S(1)} collective-permute-done((bf16[4,320]{1,0:T(4,128)(2,1)S(1)}, bf16[4,320]{1,0:T(4,128)(2,1)S(1)}, u32[]{:S(2)}, u32[]{:S(2)}) %collective-permute-start.39) | collective-permute-done | bytes 2592 | tf_op jit(solution)/shard_map/ppermute | solution.py:14
  209.0 13.8 %psum.22 = bf16[8,320]{1,0:T(8,128)(2,1)S(1)} all-reduce(f32[8,320]{1,0:T(8,128)S(1)} %dynamic_update_slice.7), channel_id=1, replica_groups=mesh['dom'=128,'blk'=4] {'blk'}, use_global_device_ids=true, to_apply=%region_12.13 | all-reduce | flops 2560 | bytes 15360 | tf_op jit(solution)/shard_map/psum | solution.py:100
  224.1 11.7 %psum.23 = f32[8]{0:T(128)} all-reduce(f32[8]{0:T(128)S(1)} %get-tuple-element.2), channel_id=1, replica_groups=mesh['dom'=128,'blk'=4] {'blk'}, use_global_device_ids=true, to_apply=%region_14.15 | all-reduce | flops 8 | bytes 64 | tf_op jit(solution)/shard_map/psum | solution.py:104
  (166 shorter events, 31.8 us)
Async XLA Ops:
  0.6 53.9 %copy-start = (bf16[32,80,320]{2,1,0:T(8,128)(2,1)S(1)}, bf16[32,80,320]{2,1,0:T(8,128)(2,1)}, u32[]{:S(2)}) copy-start(bf16[32,80,320]{2,1,0:T(8,128)(2,1)} %param.13) | copy-start | bytes 4915204
  2.9 43.4 %all-to-all-start = ((bf16[4,8,80]{2,1,0:T(8,128)(2,1)}), bf16[4,8,80]{2,1,0:T(8,128)(2,1)S(1)}, u32[]{:S(2)}, u32[]{:S(2)}) async-start(bf16[4,8,80]{2,1,0:T(8,128)(2,1)} %stack.174), calls=%async_computation | async-start | bytes 16384 | tf_op jit(solution)/shard_map/all_to_all | solution.py:19
  11.0 21.3 %collective-permute-start = (s32[4]{0:T(128)S(1)}, s32[4]{0:T(128)S(1)}, u32[]{:S(2)}, u32[]{:S(2)}) collective-permute-start(s32[4]{0:T(128)S(1)} %get-tuple-element.45), channel_id=1, source_target_pairs={{508,0},{0,4},{4,8},{8,12},{12,16},{16,20},{20,24},{24,28},{28,32}... | collective-permute-start | bytes 56 | tf_op jit(solution)/shard_map/ppermute | solution.py:14
  12.9 24.3 %collective-permute-start.1 = (s32[4]{0:T(128)S(1)}, s32[4]{0:T(128)S(1)}, u32[]{:S(2)}, u32[]{:S(2)}) collective-permute-start(s32[4]{0:T(128)S(1)} %get-tuple-element.44), channel_id=1, source_target_pairs={{504,0},{508,4},{0,8},{4,12},{8,16},{12,20},{16,24},{20,28},{24,32... | collective-permute-start | bytes 56 | tf_op jit(solution)/shard_map/ppermute | solution.py:14
  16.8 22.8 %collective-permute-start.2 = (s32[4]{0:T(128)S(1)}, s32[4]{0:T(128)S(1)}, u32[]{:S(2)}, u32[]{:S(2)}) collective-permute-start(s32[4]{0:T(128)S(1)} %get-tuple-element.43), channel_id=1, source_target_pairs={{500,0},{504,4},{508,8},{0,12},{4,16},{8,20},{12,24},{16,28},{20,3... | collective-permute-start | bytes 56 | tf_op jit(solution)/shard_map/ppermute | solution.py:14
  23.2 21.3 %collective-permute-start.3 = (s32[4]{0:T(128)S(1)}, s32[4]{0:T(128)S(1)}, u32[]{:S(2)}, u32[]{:S(2)}) collective-permute-start(s32[4]{0:T(128)S(1)} %get-tuple-element.42), channel_id=1, source_target_pairs={{496,0},{500,4},{504,8},{508,12},{0,16},{4,20},{8,24},{12,28},{16,... | collective-permute-start | bytes 56 | tf_op jit(solution)/shard_map/ppermute | solution.py:14
  28.3 16.1 %collective-permute-start.4 = (s32[4]{0:T(128)S(1)}, s32[4]{0:T(128)S(1)}, u32[]{:S(2)}, u32[]{:S(2)}) collective-permute-start(s32[4]{0:T(128)S(1)} %get-tuple-element.41), channel_id=1, source_target_pairs={{4,0},{8,4},{12,8},{16,12},{20,16},{24,20},{28,24},{32,28},{36,32}... | collective-permute-start | bytes 56 | tf_op jit(solution)/shard_map/ppermute | solution.py:14
  32.3 12.2 %collective-permute-start.5 = (s32[4]{0:T(128)S(1)}, s32[4]{0:T(128)S(1)}, u32[]{:S(2)}, u32[]{:S(2)}) collective-permute-start(s32[4]{0:T(128)S(1)} %get-tuple-element.40), channel_id=1, source_target_pairs={{8,0},{12,4},{16,8},{20,12},{24,16},{28,20},{32,24},{36,28},{40,32... | collective-permute-start | bytes 56 | tf_op jit(solution)/shard_map/ppermute | solution.py:14
  37.2 7.3 %collective-permute-start.6 = (s32[4]{0:T(128)S(1)}, s32[4]{0:T(128)S(1)}, u32[]{:S(2)}, u32[]{:S(2)}) collective-permute-start(s32[4]{0:T(128)S(1)} %get-tuple-element.39), channel_id=1, source_target_pairs={{12,0},{16,4},{20,8},{24,12},{28,16},{32,20},{36,24},{40,28},{44,3... | collective-permute-start | bytes 56 | tf_op jit(solution)/shard_map/ppermute | solution.py:14
  39.6 6.4 %collective-permute-start.7 = (s32[4]{0:T(128)S(1)}, s32[4]{0:T(128)S(1)}, u32[]{:S(2)}, u32[]{:S(2)}) collective-permute-start(s32[4]{0:T(128)S(1)} %get-tuple-element.38), channel_id=1, source_target_pairs={{16,0},{20,4},{24,8},{28,12},{32,16},{36,20},{40,24},{44,28},{48,3... | collective-permute-start | bytes 56 | tf_op jit(solution)/shard_map/ppermute | solution.py:14
  49.8 24.7 %all-to-all-start.1 = ((bf16[4,8,80]{2,1,0:T(8,128)(2,1)}), bf16[4,8,80]{2,1,0:T(8,128)(2,1)S(1)}, u32[]{:S(2)}, u32[]{:S(2)}) async-start(bf16[4,8,80]{2,1,0:T(8,128)(2,1)} %stack.193), calls=%async_computation.1 | async-start | bytes 16384 | tf_op jit(solution)/shard_map/all_to_all | solution.py:19
  56.6 19.2 %collective-permute-start.8 = (f32[4,320]{1,0:T(4,128)S(1)}, f32[4,320]{1,0:T(4,128)S(1)}, u32[]{:S(2)}, u32[]{:S(2)}) collective-permute-start(f32[4,320]{1,0:T(4,128)S(1)} %get-tuple-element.21), channel_id=1, source_target_pairs={{508,0},{0,4},{4,8},{8,12},{12,16},{16,20},{20,24},{24,28},{28,32}... | collective-permute-start | bytes 15368 | tf_op jit(solution)/shard_map/ppermute | solution.py:14
  58.5 21.7 %collective-permute-start.9 = (f32[4,320]{1,0:T(4,128)S(1)}, f32[4,320]{1,0:T(4,128)S(1)}, u32[]{:S(2)}, u32[]{:S(2)}) collective-permute-start(f32[4,320]{1,0:T(4,128)S(1)} %get-tuple-element.20), channel_id=1, source_target_pairs={{504,0},{508,4},{0,8},{4,12},{8,16},{12,20},{16,24},{20,28},{24,32... | collective-permute-start | bytes 15368 | tf_op jit(solution)/shard_map/ppermute | solution.py:14
  63.0 19.2 %collective-permute-start.10 = (f32[4,320]{1,0:T(4,128)S(1)}, f32[4,320]{1,0:T(4,128)S(1)}, u32[]{:S(2)}, u32[]{:S(2)}) collective-permute-start(f32[4,320]{1,0:T(4,128)S(1)} %get-tuple-element.19), channel_id=1, source_target_pairs={{500,0},{504,4},{508,8},{0,12},{4,16},{8,20},{12,24},{16,28},{20,3... | collective-permute-start | bytes 15368 | tf_op jit(solution)/shard_map/ppermute | solution.py:14
  66.6 19.1 %collective-permute-start.11 = (f32[4,320]{1,0:T(4,128)S(1)}, f32[4,320]{1,0:T(4,128)S(1)}, u32[]{:S(2)}, u32[]{:S(2)}) collective-permute-start(f32[4,320]{1,0:T(4,128)S(1)} %get-tuple-element.18), channel_id=1, source_target_pairs={{496,0},{500,4},{504,8},{508,12},{0,16},{4,20},{8,24},{12,28},{16,... | collective-permute-start | bytes 15368 | tf_op jit(solution)/shard_map/ppermute | solution.py:14
  72.5 18.1 %collective-permute-start.12 = (f32[4,320]{1,0:T(4,128)S(1)}, f32[4,320]{1,0:T(4,128)S(1)}, u32[]{:S(2)}, u32[]{:S(2)}) collective-permute-start(f32[4,320]{1,0:T(4,128)S(1)} %get-tuple-element.17), channel_id=1, source_target_pairs={{4,0},{8,4},{12,8},{16,12},{20,16},{24,20},{28,24},{32,28},{36,32}... | collective-permute-start | bytes 15368 | tf_op jit(solution)/shard_map/ppermute | solution.py:14
  75.8 60.8 %copy-start.3 = (bf16[8,80,320]{2,1,0:T(8,128)(2,1)S(1)}, bf16[8,80,320]{2,1,0:T(8,128)(2,1)}, u32[]{:S(2)}) copy-start(bf16[8,80,320]{2,1,0:T(8,128)(2,1)} %param.15) | copy-start | bytes 1228804
  75.8 18.1 %collective-permute-start.13 = (f32[4,320]{1,0:T(4,128)S(1)}, f32[4,320]{1,0:T(4,128)S(1)}, u32[]{:S(2)}, u32[]{:S(2)}) collective-permute-start(f32[4,320]{1,0:T(4,128)S(1)} %get-tuple-element.16), channel_id=1, source_target_pairs={{8,0},{12,4},{16,8},{20,12},{24,16},{28,20},{32,24},{36,28},{40,32... | collective-permute-start | bytes 15368 | tf_op jit(solution)/shard_map/ppermute | solution.py:14
  80.2 17.1 %collective-permute-start.14 = (f32[4,320]{1,0:T(4,128)S(1)}, f32[4,320]{1,0:T(4,128)S(1)}, u32[]{:S(2)}, u32[]{:S(2)}) collective-permute-start(f32[4,320]{1,0:T(4,128)S(1)} %get-tuple-element.15), channel_id=1, source_target_pairs={{12,0},{16,4},{20,8},{24,12},{28,16},{32,20},{36,24},{40,28},{44,3... | collective-permute-start | bytes 15368 | tf_op jit(solution)/shard_map/ppermute | solution.py:14
  82.2 17.3 %collective-permute-start.15 = (f32[4,320]{1,0:T(4,128)S(1)}, f32[4,320]{1,0:T(4,128)S(1)}, u32[]{:S(2)}, u32[]{:S(2)}) collective-permute-start(f32[4,320]{1,0:T(4,128)S(1)} %get-tuple-element.14), channel_id=1, source_target_pairs={{16,0},{20,4},{24,8},{28,12},{32,16},{36,20},{40,24},{44,28},{48,3... | collective-permute-start | bytes 15368 | tf_op jit(solution)/shard_map/ppermute | solution.py:14
  85.8 16.8 %collective-permute-start.16 = (bf16[4,320]{1,0:T(4,128)(2,1)S(1)}, bf16[4,320]{1,0:T(4,128)(2,1)S(1)}, u32[]{:S(2)}, u32[]{:S(2)}) collective-permute-start(bf16[4,320]{1,0:T(4,128)(2,1)S(1)} %get-tuple-element.37), channel_id=1, source_target_pairs={{4,0},{8,4},{12,8},{16,12},{20,16},{24,20},{28,24},{32,28},{36,32}... | collective-permute-start | bytes 7688 | tf_op jit(solution)/shard_map/ppermute | solution.py:14
  90.5 15.6 %collective-permute-start.17 = (bf16[4,320]{1,0:T(4,128)(2,1)S(1)}, bf16[4,320]{1,0:T(4,128)(2,1)S(1)}, u32[]{:S(2)}, u32[]{:S(2)}) collective-permute-start(bf16[4,320]{1,0:T(4,128)(2,1)S(1)} %get-tuple-element.36), channel_id=1, source_target_pairs={{8,0},{12,4},{16,8},{20,12},{24,16},{28,20},{32,24},{36,28},{40,32... | collective-permute-start | bytes 7688 | tf_op jit(solution)/shard_map/ppermute | solution.py:14
  93.9 16.4 %collective-permute-start.18 = (bf16[4,320]{1,0:T(4,128)(2,1)S(1)}, bf16[4,320]{1,0:T(4,128)(2,1)S(1)}, u32[]{:S(2)}, u32[]{:S(2)}) collective-permute-start(bf16[4,320]{1,0:T(4,128)(2,1)S(1)} %get-tuple-element.35), channel_id=1, source_target_pairs={{12,0},{16,4},{20,8},{24,12},{28,16},{32,20},{36,24},{40,28},{44,3... | collective-permute-start | bytes 7688 | tf_op jit(solution)/shard_map/ppermute | solution.py:14
  97.3 15.2 %collective-permute-start.19 = (bf16[4,320]{1,0:T(4,128)(2,1)S(1)}, bf16[4,320]{1,0:T(4,128)(2,1)S(1)}, u32[]{:S(2)}, u32[]{:S(2)}) collective-permute-start(bf16[4,320]{1,0:T(4,128)(2,1)S(1)} %get-tuple-element.34), channel_id=1, source_target_pairs={{16,0},{20,4},{24,8},{28,12},{32,16},{36,20},{40,24},{44,28},{48,3... | collective-permute-start | bytes 7688 | tf_op jit(solution)/shard_map/ppermute | solution.py:14
  99.6 12.9 %collective-permute-start.20 = (bf16[4,320]{1,0:T(4,128)(2,1)S(1)}, bf16[4,320]{1,0:T(4,128)(2,1)S(1)}, u32[]{:S(2)}, u32[]{:S(2)}) collective-permute-start(bf16[4,320]{1,0:T(4,128)(2,1)S(1)} %get-tuple-element.33), channel_id=1, source_target_pairs={{508,0},{0,4},{4,8},{8,12},{12,16},{16,20},{20,24},{24,28},{28,32}... | collective-permute-start | bytes 7688 | tf_op jit(solution)/shard_map/ppermute | solution.py:14
  101.6 35.2 %copy-start.1 = (f32[8,80]{1,0:T(8,128)S(1)}, f32[8,80]{1,0:T(8,128)}, u32[]{:S(2)}) copy-start(f32[8,80]{1,0:T(8,128)} %param.14) | copy-start | bytes 7684
  102.5 10.0 %collective-permute-start.21 = (bf16[4,320]{1,0:T(4,128)(2,1)S(1)}, bf16[4,320]{1,0:T(4,128)(2,1)S(1)}, u32[]{:S(2)}, u32[]{:S(2)}) collective-permute-start(bf16[4,320]{1,0:T(4,128)(2,1)S(1)} %get-tuple-element.32), channel_id=1, source_target_pairs={{504,0},{508,4},{0,8},{4,12},{8,16},{12,20},{16,24},{20,28},{24,32... | collective-permute-start | bytes 7688 | tf_op jit(solution)/shard_map/ppermute | solution.py:14
  106.2 9.1 %collective-permute-start.22 = (bf16[4,320]{1,0:T(4,128)(2,1)S(1)}, bf16[4,320]{1,0:T(4,128)(2,1)S(1)}, u32[]{:S(2)}, u32[]{:S(2)}) collective-permute-start(bf16[4,320]{1,0:T(4,128)(2,1)S(1)} %get-tuple-element.31), channel_id=1, source_target_pairs={{500,0},{504,4},{508,8},{0,12},{4,16},{8,20},{12,24},{16,28},{20,3... | collective-permute-start | bytes 7688 | tf_op jit(solution)/shard_map/ppermute | solution.py:14
  110.4 9.7 %collective-permute-start.23 = (bf16[4,320]{1,0:T(4,128)(2,1)S(1)}, bf16[4,320]{1,0:T(4,128)(2,1)S(1)}, u32[]{:S(2)}, u32[]{:S(2)}) collective-permute-start(bf16[4,320]{1,0:T(4,128)(2,1)S(1)} %get-tuple-element.30), channel_id=1, source_target_pairs={{496,0},{500,4},{504,8},{508,12},{0,16},{4,20},{8,24},{12,28},{16,... | collective-permute-start | bytes 7688 | tf_op jit(solution)/shard_map/ppermute | solution.py:14
  139.4 18.9 %all-to-all-start.2 = ((bf16[4,8,80]{2,1,0:T(8,128)(2,1)}), bf16[4,8,80]{2,1,0:T(8,128)(2,1)S(1)}, u32[]{:S(2)}, u32[]{:S(2)}) async-start(bf16[4,8,80]{2,1,0:T(8,128)(2,1)} %stack.221), calls=%async_computation.2 | async-start | bytes 16384 | tf_op jit(solution)/shard_map/all_to_all | solution.py:19
  146.9 12.8 %collective-permute-start.24 = (f32[4,320]{1,0:T(4,128)S(1)}, f32[4,320]{1,0:T(4,128)S(1)}, u32[]{:S(2)}, u32[]{:S(2)}) collective-permute-start(f32[4,320]{1,0:T(4,128)S(1)} %get-tuple-element.13), channel_id=1, source_target_pairs={{508,0},{0,4},{4,8},{8,12},{12,16},{16,20},{20,24},{24,28},{28,32}... | collective-permute-start | bytes 15368 | tf_op jit(solution)/shard_map/ppermute | solution.py:14
  148.8 17.8 %collective-permute-start.25 = (f32[4,320]{1,0:T(4,128)S(1)}, f32[4,320]{1,0:T(4,128)S(1)}, u32[]{:S(2)}, u32[]{:S(2)}) collective-permute-start(f32[4,320]{1,0:T(4,128)S(1)} %get-tuple-element.12), channel_id=1, source_target_pairs={{504,0},{508,4},{0,8},{4,12},{8,16},{12,20},{16,24},{20,28},{24,32... | collective-permute-start | bytes 15368 | tf_op jit(solution)/shard_map/ppermute | solution.py:14
  150.7 19.1 %collective-permute-start.26 = (f32[4,320]{1,0:T(4,128)S(1)}, f32[4,320]{1,0:T(4,128)S(1)}, u32[]{:S(2)}, u32[]{:S(2)}) collective-permute-start(f32[4,320]{1,0:T(4,128)S(1)} %get-tuple-element.11), channel_id=1, source_target_pairs={{500,0},{504,4},{508,8},{0,12},{4,16},{8,20},{12,24},{16,28},{20,3... | collective-permute-start | bytes 15368 | tf_op jit(solution)/shard_map/ppermute | solution.py:14
  152.7 22.0 %collective-permute-start.27 = (f32[4,320]{1,0:T(4,128)S(1)}, f32[4,320]{1,0:T(4,128)S(1)}, u32[]{:S(2)}, u32[]{:S(2)}) collective-permute-start(f32[4,320]{1,0:T(4,128)S(1)} %get-tuple-element.10), channel_id=1, source_target_pairs={{496,0},{500,4},{504,8},{508,12},{0,16},{4,20},{8,24},{12,28},{16,... | collective-permute-start | bytes 15368 | tf_op jit(solution)/shard_map/ppermute | solution.py:14
  154.6 23.4 %collective-permute-start.28 = (f32[4,320]{1,0:T(4,128)S(1)}, f32[4,320]{1,0:T(4,128)S(1)}, u32[]{:S(2)}, u32[]{:S(2)}) collective-permute-start(f32[4,320]{1,0:T(4,128)S(1)} %get-tuple-element.9), channel_id=1, source_target_pairs={{4,0},{8,4},{12,8},{16,12},{20,16},{24,20},{28,24},{32,28},{36,32}... | collective-permute-start | bytes 15368 | tf_op jit(solution)/shard_map/ppermute | solution.py:14
  159.6 20.9 %collective-permute-start.29 = (f32[4,320]{1,0:T(4,128)S(1)}, f32[4,320]{1,0:T(4,128)S(1)}, u32[]{:S(2)}, u32[]{:S(2)}) collective-permute-start(f32[4,320]{1,0:T(4,128)S(1)} %get-tuple-element.8), channel_id=1, source_target_pairs={{8,0},{12,4},{16,8},{20,12},{24,16},{28,20},{32,24},{36,28},{40,32... | collective-permute-start | bytes 15368 | tf_op jit(solution)/shard_map/ppermute | solution.py:14
  166.6 15.8 %collective-permute-start.30 = (f32[4,320]{1,0:T(4,128)S(1)}, f32[4,320]{1,0:T(4,128)S(1)}, u32[]{:S(2)}, u32[]{:S(2)}) collective-permute-start(f32[4,320]{1,0:T(4,128)S(1)} %get-tuple-element.7), channel_id=1, source_target_pairs={{12,0},{16,4},{20,8},{24,12},{28,16},{32,20},{36,24},{40,28},{44,3... | collective-permute-start | bytes 15368 | tf_op jit(solution)/shard_map/ppermute | solution.py:14
  169.9 14.8 %collective-permute-start.31 = (f32[4,320]{1,0:T(4,128)S(1)}, f32[4,320]{1,0:T(4,128)S(1)}, u32[]{:S(2)}, u32[]{:S(2)}) collective-permute-start(f32[4,320]{1,0:T(4,128)S(1)} %get-tuple-element.6), channel_id=1, source_target_pairs={{16,0},{20,4},{24,8},{28,12},{32,16},{36,20},{40,24},{44,28},{48,3... | collective-permute-start | bytes 15368 | tf_op jit(solution)/shard_map/ppermute | solution.py:14
  174.7 12.9 %collective-permute-start.32 = (bf16[4,320]{1,0:T(4,128)(2,1)S(1)}, bf16[4,320]{1,0:T(4,128)(2,1)S(1)}, u32[]{:S(2)}, u32[]{:S(2)}) collective-permute-start(bf16[4,320]{1,0:T(4,128)(2,1)S(1)} %get-tuple-element.29), channel_id=1, source_target_pairs={{4,0},{8,4},{12,8},{16,12},{20,16},{24,20},{28,24},{32,28},{36,32}... | collective-permute-start | bytes 7688 | tf_op jit(solution)/shard_map/ppermute | solution.py:14
  178.0 13.3 %collective-permute-start.33 = (bf16[4,320]{1,0:T(4,128)(2,1)S(1)}, bf16[4,320]{1,0:T(4,128)(2,1)S(1)}, u32[]{:S(2)}, u32[]{:S(2)}) collective-permute-start(bf16[4,320]{1,0:T(4,128)(2,1)S(1)} %get-tuple-element.28), channel_id=1, source_target_pairs={{8,0},{12,4},{16,8},{20,12},{24,16},{28,20},{32,24},{36,28},{40,32... | collective-permute-start | bytes 7688 | tf_op jit(solution)/shard_map/ppermute | solution.py:14
  180.5 16.2 %collective-permute-start.34 = (bf16[4,320]{1,0:T(4,128)(2,1)S(1)}, bf16[4,320]{1,0:T(4,128)(2,1)S(1)}, u32[]{:S(2)}, u32[]{:S(2)}) collective-permute-start(bf16[4,320]{1,0:T(4,128)(2,1)S(1)} %get-tuple-element.27), channel_id=1, source_target_pairs={{12,0},{16,4},{20,8},{24,12},{28,16},{32,20},{36,24},{40,28},{44,3... | collective-permute-start | bytes 7688 | tf_op jit(solution)/shard_map/ppermute | solution.py:14
  182.5 17.6 %collective-permute-start.35 = (bf16[4,320]{1,0:T(4,128)(2,1)S(1)}, bf16[4,320]{1,0:T(4,128)(2,1)S(1)}, u32[]{:S(2)}, u32[]{:S(2)}) collective-permute-start(bf16[4,320]{1,0:T(4,128)(2,1)S(1)} %get-tuple-element.26), channel_id=1, source_target_pairs={{16,0},{20,4},{24,8},{28,12},{32,16},{36,20},{40,24},{44,28},{48,3... | collective-permute-start | bytes 7688 | tf_op jit(solution)/shard_map/ppermute | solution.py:14
  184.7 15.4 %collective-permute-start.36 = (bf16[4,320]{1,0:T(4,128)(2,1)S(1)}, bf16[4,320]{1,0:T(4,128)(2,1)S(1)}, u32[]{:S(2)}, u32[]{:S(2)}) collective-permute-start(bf16[4,320]{1,0:T(4,128)(2,1)S(1)} %get-tuple-element.25), channel_id=1, source_target_pairs={{508,0},{0,4},{4,8},{8,12},{12,16},{16,20},{20,24},{24,28},{28,32}... | collective-permute-start | bytes 7688 | tf_op jit(solution)/shard_map/ppermute | solution.py:14
  186.8 36.5 %copy-start.2 = (f32[8,80]{1,0:T(8,128)S(1)}, f32[8,80]{1,0:T(8,128)}, u32[]{:S(2)}) copy-start(f32[8,80]{1,0:T(8,128)} %param.17) | copy-start | bytes 7684
  187.7 12.4 %collective-permute-start.37 = (bf16[4,320]{1,0:T(4,128)(2,1)S(1)}, bf16[4,320]{1,0:T(4,128)(2,1)S(1)}, u32[]{:S(2)}, u32[]{:S(2)}) collective-permute-start(bf16[4,320]{1,0:T(4,128)(2,1)S(1)} %get-tuple-element.24), channel_id=1, source_target_pairs={{504,0},{508,4},{0,8},{4,12},{8,16},{12,20},{16,24},{20,28},{24,32... | collective-permute-start | bytes 7688 | tf_op jit(solution)/shard_map/ppermute | solution.py:14
  191.3 9.1 %collective-permute-start.38 = (bf16[4,320]{1,0:T(4,128)(2,1)S(1)}, bf16[4,320]{1,0:T(4,128)(2,1)S(1)}, u32[]{:S(2)}, u32[]{:S(2)}) collective-permute-start(bf16[4,320]{1,0:T(4,128)(2,1)S(1)} %get-tuple-element.23), channel_id=1, source_target_pairs={{500,0},{504,4},{508,8},{0,12},{4,16},{8,20},{12,24},{16,28},{20,3... | collective-permute-start | bytes 7688 | tf_op jit(solution)/shard_map/ppermute | solution.py:14
  196.7 9.7 %collective-permute-start.39 = (bf16[4,320]{1,0:T(4,128)(2,1)S(1)}, bf16[4,320]{1,0:T(4,128)(2,1)S(1)}, u32[]{:S(2)}, u32[]{:S(2)}) collective-permute-start(bf16[4,320]{1,0:T(4,128)(2,1)S(1)} %get-tuple-element.22), channel_id=1, source_target_pairs={{496,0},{500,4},{504,8},{508,12},{0,16},{4,20},{8,24},{12,28},{16,... | collective-permute-start | bytes 7688 | tf_op jit(solution)/shard_map/ppermute | solution.py:14
